TPU v7x, 256 devices: a whole 4x4x8 slice. The times are simulated.
256 devices in a mesh: group: 16 (over z, core), tok: 4 (over y), head: 4 (over x).
Axes of the slice: x: 4, y: 4, z: 8, core: 2. Of those that a mesh axis runs over, the one named last changes fastest.
Arguments:
- streams: bfloat16 [2, 32768, 2240], P(None, ('group', 'tok'), 'head'), may hold values from -6 to 6
- w_query: bfloat16 [2240, 2240], P(None, 'head'), may hold values from -0.125 to 0.125
- w_key: bfloat16 [2240, 2240], P(None, 'head'), may hold values from -0.125 to 0.125
- w_value: bfloat16 [2240, 2240], P(None, 'head'), may hold values from -0.125 to 0.125
- gain: float32 [2240], P('head'), may hold values from 0.25 to 1.75
Outputs:
- attended: bfloat16 [2, 32768, 2240], P(None, ('group', 'tok'), 'head')
All inputs are finite; a program needn't handle non-finite values.
Results may differ from a plain program's by a relative error of at most 0.0053.
Values may be sent and summed in bfloat16 or wider, within the bound.
A program may use at most 64 MiB of HBM per device.

v0:
```python
import jax
import jax.numpy as jnp
from jax import lax
from jax.sharding import PartitionSpec as P

HEAD_DIM = 112


def entering(value, axis, join, neutral):
    count, mine = (lax.axis_size(axis), lax.axis_index(axis))
    pieces = lax.all_gather(value, axis)
    total = jnp.full_like(value, 0) + jnp.asarray(neutral, value.dtype)

    def lap(position, total):
        longer = join(total, pieces[position])
        return jnp.where(position < mine, longer, total)

    return lax.fori_loop(0, count - 1, lap, total)


def add_states(earlier, later):
    return earlier + later


def local(streams, w_query, w_key, w_value, gain):
    width_dev = w_query.shape[1]
    heads_dev = width_dev // HEAD_DIM
    token_count = streams.shape[1]
    blank_sums = jnp.zeros((2, token_count, width_dev), jnp.float32)
    running = (blank_sums, blank_sums, blank_sums)
    pieces = lax.all_gather(streams, "head", axis=2, tiled=True)
    results = []
    for total, matrix in zip(running, (w_query, w_key, w_value)):
        results.append(
            jnp.einsum("std,dw->stw", pieces, matrix, preferred_element_type=jnp.float32)
        )
    query_sum, key_sum, value_sum = tuple(results)
    query = query_sum.astype(jnp.bfloat16)
    key_relu = jnp.maximum(key_sum.astype(jnp.bfloat16), 0).reshape(
        2, token_count, heads_dev, HEAD_DIM
    )
    value_heads = value_sum.astype(jnp.bfloat16).reshape(2, token_count, heads_dev, HEAD_DIM)
    states = jnp.einsum(
        "stha,sthb->sahb", key_relu, value_heads, preferred_element_type=jnp.float32
    )
    states = states.reshape(2, HEAD_DIM, width_dev)
    clean_part = states[0:1]
    noisy_part = states[1:2]
    empty_state = jnp.zeros_like(clean_part)
    clean_total, noisy_total = lax.psum((clean_part, noisy_part), "tok")
    prefix = entering(clean_total, "group", add_states, empty_state)
    totals = jnp.concatenate([prefix + clean_total, prefix + noisy_total], axis=0)
    totals = totals.reshape(2, HEAD_DIM, heads_dev, HEAD_DIM)
    query_relu = (
        jnp.maximum(query, 0).astype(jnp.float32).reshape(2, token_count, heads_dev, HEAD_DIM)
    )
    reading = jnp.einsum("stha,sahb->sthb", query_relu, totals, precision=lax.Precision.HIGHEST)
    scale = lax.rsqrt(jnp.mean(reading * reading, axis=-1, keepdims=True) + 1e-06)
    normed = reading * scale * gain.reshape(heads_dev, HEAD_DIM)
    return normed.reshape(2, token_count, width_dev).astype(jnp.bfloat16)


def solution(mesh):
    return jax.shard_map(
        local,
        mesh=mesh,
        in_specs=(
            P(None, ("group", "tok"), "head"),
            P(None, "head"),
            P(None, "head"),
            P(None, "head"),
            P("head"),
        ),
        out_specs=P(None, ("group", "tok"), "head"),
        check_vma=False,
    )
```

profile of v0, /device:TPU:32, one launch (start us, length us, event | category | flops | bytes accessed | tf_op | source)
XLA Modules:
  0.0 197.0 jit_solution(7859422837325611413)
XLA Ops:
  6.5 0.0 copy-start
  6.5 0.0 all-gather.4.cloned.1.call-start
  6.5 0.7 all-gather.4.cloned.1.call-update
  7.3 0.0 all-reduce.3.cloned.1.call-start
  7.3 58.5 %all-gather.4.cloned.1.call-done = bf16[2,512,2240]{1,2,0:T(8,128)(2,1)} async-done(((bf16[2,512,560]{1,2,0:T(8,128)(2,1)}), bf16[2,512,2240]{1,2,0:T(8,128)(2,1)}) %all-gather.4.cloned.1.call-update) | async-done | bytes 4587536 | tf_op jit(solution)/shard_map/all_gather | solution.py:31
  65.8 0.0 copy-done
  65.8 0.0 copy-start.4
  65.8 0.0 copy-start.5
  65.8 5.3 %fusion.9 = bf16[2,512,560]{1,2,0:T(8,128)(2,1)S(1)} fusion(bf16[2,512,2240]{1,2,0:T(8,128)(2,1)} %all-gather.4.cloned.1.call-done, bf16[2240,560]{0,1:T(8,128)(2,1)S(1)} %copy-done), kind=kOutput, calls=%fused_computation.12 | convolution fusion | flops 2569584640 | bytes 8243200 | tf_op jit(solution)/shard_map/std,dw->stw/dot_general | solution.py:35
  71.1 0.0 copy-done.4
  71.1 0.0 copy-done.5
  71.1 2.8 %fusion.21 = bf16[2,512,560]{1,2,0:T(8,128)(2,1)S(1)} fusion(bf16[2,512,2240]{1,2,0:T(8,128)(2,1)S(1)} %copy-done.4, bf16[2240,560]{0,1:T(8,128)(2,1)S(1)} %copy-done.5), kind=kOutput, calls=%fused_computation.16 | convolution fusion | flops 2570158080 | bytes 8243200 | tf_op jit(solution)/shard_map/std,dw->stw/dot_general | solution.py:35
  73.9 0.5 convolution_bitcast_fusion
  74.4 0.0 copy-start.3
  74.4 0.9 copy.12
  75.3 0.9 copy.10
  76.2 0.0 all-reduce.3.cloned.1.call-update
  76.2 0.0 all-gather.6.cloned.1.call-start
  76.2 49.1 %all-reduce.3.cloned.1.call-done = (f32[1,112,560]{2,1,0:T(8,128)}, f32[1,112,560]{2,1,0:T(8,128)}) async-done(((f32[1,112,560]{2,1,0:T(8,128)}, f32[1,112,560]{2,1,0:T(8,128)}), (f32[1,112,560]{2,1,0:T(8,128)}, f32[1,112,560]{2,1,0:T(8,128)})) %all-reduce.3.cloned.1.call-update) | async-done | bytes 501776 | tf_op jit(solution)/shard_map/psum | solution.py:50
  125.3 0.0 all-gather.6.cloned.1.call-update
  125.4 0.0 copy-done.3
  125.4 0.1 mul.24
  125.5 6.9 %fusion.18 = bf16[2,512,560]{1,2,0:T(8,128)(2,1)} fusion(bf16[2,512,2240]{1,2,0:T(8,128)(2,1)} %all-gather.4.cloned.1.call-done, bf16[2240,560]{0,1:T(8,128)(2,1)} %param.8), kind=kOutput, calls=%fused_computation.15 | convolution fusion | flops 2570158080 | bytes 8243200 | tf_op jit(solution)/shard_map/std,dw->stw/dot_general | solution.py:35
  132.4 0.0 copy-start.1
  132.4 0.0 copy-start.2
  132.4 37.0 %all-gather.6.cloned.1.call-done = f32[16,112,560]{2,1,0:T(8,128)} async-done(((f32[1,112,560]{2,1,0:T(8,128)}), f32[16,112,560]{2,1,0:T(8,128)}) %all-gather.6.cloned.1.call-update) | async-done | bytes 4014096 | tf_op jit(solution)/shard_map/all_gather | solution.py:11
  169.4 15.9 %while.14 = (s32[]{:T(128)}, f32[1,112,560]{2,1,0:T(8,128)S(1)}, s32[]{:T(128)}, f32[16,1,112,560]{3,2,1,0:T(8,128)}, s32[]{:T(128)}, /*index=5*/s32[]{:T(128)}) while((s32[]{:T(128)}, f32[1,112,560]{2,1,0:T(8,128)S(1)}, s32[]{:T(128)}, f32[16,1,112,560]{3,2,1,0:T(8,128)}, s32[]{:T(128)}, /*index=5*/s32[]{:T(128)}) %tuple.47), condition=%wide.region_2.3_spmd.clone, body=%wide.region_1.0_spmd.clone.sunk | while | flops 188164 | bytes 752741 | solution.py:18
  169.4 1.0 add_select_fusion.2
  170.5 1.0 add_select_fusion.2
  171.6 1.0 add_select_fusion.2
  172.6 1.0 add_select_fusion.2
  173.7 1.0 add_select_fusion.2
  174.8 1.0 add_select_fusion.2
  175.8 1.0 add_select_fusion.2
  176.9 1.0 add_select_fusion.2
  177.9 1.0 add_select_fusion.2
  179.0 1.0 add_select_fusion.2
  180.1 1.0 add_select_fusion.2
  181.1 1.0 add_select_fusion.2
  182.2 1.0 add_select_fusion.2
  183.3 1.0 add_select_fusion.2
  184.3 1.0 add_select_fusion.2
  185.4 0.0 copy-done.1
  185.4 0.0 copy-done.2
  185.4 0.1 fusion.25
  185.5 1.1 copy.13
  186.6 2.6 %fusion.6 = (f32[2,512,5]{1,2,0:T(8,128)S(1)}, f32[2,5,112,512]{3,2,1,0:T(8,128)S(1)}) fusion(f32[2,112,5,112]{1,3,2,0:T(8,128)} %bitcast.51, bf16[2,512,5,112]{1,3,2,0:T(8,128)(2,1)} %bitcast.56), kind=kOutput, calls=%fused_computation.9 | convolution fusion | flops 771845120 | bytes 3962880 | tf_op jit(solution)/shard_map/stha,sahb->sthb/dot_general | solution.py:57
  189.2 1.3 fusion.8
  (4 shorter events, 0.1 us)
Async XLA Ops:
  6.5 59.2 %copy-start = (bf16[2240,560]{0,1:T(8,128)(2,1)S(1)}, bf16[2240,560]{0,1:T(8,128)(2,1)}, u32[]{:S(2)}) copy-start(bf16[2240,560]{0,1:T(8,128)(2,1)} %param.10) | copy-start | bytes 7526404
  6.5 59.2 %all-gather.4.cloned.1.call-start = ((), (), s32[]{:S(2)}) async-start(), calls=%async_computation | async-start | bytes 5734400 | tf_op jit(solution)/shard_map/all_gather | solution.py:31
  7.3 118.1 %all-reduce.3.cloned.1.call-start = ((), (), s32[]{:S(2)}) async-start(), calls=%async_computation.2 | async-start | bytes 1146880 | tf_op jit(solution)/shard_map/psum | solution.py:50
  65.8 5.3 %copy-start.4 = (bf16[2,512,2240]{1,2,0:T(8,128)(2,1)S(1)}, bf16[2,512,2240]{1,2,0:T(8,128)(2,1)}, u32[]{:S(2)}) copy-start(bf16[2,512,2240]{1,2,0:T(8,128)(2,1)} %all-gather.4.cloned.1.call-done) | copy-start | bytes 13762564
  65.8 5.3 %copy-start.5 = (bf16[2240,560]{0,1:T(8,128)(2,1)S(1)}, bf16[2240,560]{0,1:T(8,128)(2,1)}, u32[]{:S(2)}) copy-start(bf16[2240,560]{0,1:T(8,128)(2,1)} %param.9) | copy-start | bytes 7526404
  74.4 51.0 %copy-start.3 = (f32[560]{0:T(1024)S(1)}, f32[560]{0:T(1024)}, u32[]{:S(2)}) copy-start(f32[560]{0:T(1024)} %param.11) | copy-start | bytes 6724
  76.2 93.3 %all-gather.6.cloned.1.call-start = ((), (), s32[]{:S(2)}) async-start(), calls=%async_computation.1 | async-start | bytes 4874240 | tf_op jit(solution)/shard_map/all_gather | solution.py:11
  132.4 53.0 %copy-start.1 = (f32[1,112,560]{2,1,0:T(8,128)S(1)}, f32[1,112,560]{2,1,0:T(8,128)}, u32[]{:S(2)}) copy-start(f32[1,112,560]{2,1,0:T(8,128)} %get-tuple-element.116) | copy-start | bytes 752644
  132.4 53.0 %copy-start.2 = (f32[1,112,560]{2,1,0:T(8,128)S(1)}, f32[1,112,560]{2,1,0:T(8,128)}, u32[]{:S(2)}) copy-start(f32[1,112,560]{2,1,0:T(8,128)} %get-tuple-element.117) | copy-start | bytes 752644
Sparse Core Ops, SparseCore 0:
  9.1 56.5 all-gather.3
  76.3 48.9 all-reduce.2
  127.2 42.2 all-gather.5
where the time goes:
time: 199 us; the launch traced here: 197 us
  waiting for transfers between devices  145 us (73%)
  matrix products  18 us (9%)
  other arithmetic  17 us (9%)
  between operations  13.2 us (7%)
  local copies, waits for them, and re-layouts  2.93 us (1%)
    all_gather x1, waiting for transfers between devices, local(): pieces = lax.all_gather(streams, 'head', axis=2, tiled=True)  58.5 us
    psum x1, waiting for transfers between devices, local(): clean_total, noisy_total = lax.psum((clean_part, noisy_part), 'tok')  49.1 us
    all_gather x1, waiting for transfers between devices, entering(): pieces = lax.all_gather(value, axis)  37 us
    select_n x15, other arithmetic, lap(): return jnp.where(position < mine, longer, total)  15.6 us
    dot_general x3, matrix products, local(): jnp.einsum('std,dw->stw', pieces, matrix, preferred_element_type=jnp.floa...  15 us
  transfers between devices with their start and end apart: 3, of which 3 were waited for; matrix products, arithmetic and copies ran while one was open for 4% of the time, Pallas kernels for 0%

commit v1 on v0

v1 whole, which is shorter than its diff:
```python
import functools

import jax
import jax.numpy as jnp
from jax import lax
from jax.experimental import pallas as pl
from jax.experimental.pallas import tpu as pltpu
from jax.sharding import PartitionSpec as P

MESH = pl.DeviceIdType.MESH
F32 = jnp.float32
BF16 = jnp.bfloat16

HD = 112
LN = 128
NH = 5
NX = 4
NY = 4
NZ = 8
DW = 560
MAIN = 512
TAIL = 48
TOK = 512
ROWS = 2 * TOK
CH = 128
NC = ROWS // CH
KW = NX * MAIN + NX * 64
PW = NH * LN
QR = PW // NY
ER = QR // 2


def rcopy(src, dst, ssem, rsem, where):
    return pltpu.make_async_remote_copy(
        src_ref=src, dst_ref=dst, send_sem=ssem, recv_sem=rsem, device_id=where, device_id_type=MESH
    )


def kernel(
    streams, wq, wk, wv, gain, out,
    raw, wcat, stage, xbuf, tbuf, qkv, obuf, st32, st16, rsbuf, cst, csend, crecv,
    zsend, zrecv, psend, precv, pfx, tot,
    lsem, wsem, osem, xs, xr, fs, fr, ts, tr, us, ur, ys, yr, cs, cr, zs, zr,
):
    x = lax.axis_index("head")
    y = lax.axis_index("tok")
    g = lax.axis_index("group")
    z, core = g // 2, g % 2
    right, left = (x + 1) % NX, (x + NX - 1) % NX
    mate = g + 1 - 2 * core
    side = (right, left)

    barrier = pltpu.get_barrier_semaphore()
    partners = [{"head": right}, {"head": left}, {"group": mate}]
    partners += [{"tok": (y + d) % NY} for d in range(1, NY)]
    partners += [{"group": ((z + d) % NZ) * 2 + core} for d in range(1, NZ)]
    for where in partners:
        pl.semaphore_signal(barrier, inc=1, device_id=where, device_id_type=MESH)

    stage_copy = pltpu.make_async_copy(streams, stage, lsem.at[0])
    stage_copy.start()

    def cols(i):
        return pl.ds(pl.multiple_of(i * MAIN, MAIN), MAIN)

    own = [
        pltpu.make_async_copy(
            streams.at[s, :, pl.ds(0, MAIN)], xbuf.at[pl.ds(s * TOK, TOK), cols(x)], lsem.at[1 + s]
        )
        for s in range(2)
    ]
    for c in own:
        c.start()
    wcopies = []
    for p, w in enumerate((wk, wq, wv)):
        for i in range(NX):
            wcopies.append(
                pltpu.make_async_copy(
                    w.at[pl.ds(i * DW, MAIN), :], raw.at[p, pl.ds(i * MAIN, MAIN), :], wsem.at[p, i]
                )
            )
            wcopies.append(
                pltpu.make_async_copy(
                    w.at[pl.ds(i * DW + MAIN, TAIL), :],
                    raw.at[p, pl.ds(NX * MAIN + i * 64, TAIL), :],
                    wsem.at[p, NX + i],
                )
            )
    for c in wcopies:
        c.start()

    pl.semaphore_wait(barrier, len(partners))

    def main_copy(d, c):
        s, t = c // (NC // 2), (c % (NC // 2)) * CH
        return rcopy(
            streams.at[s, pl.ds(t, CH), pl.ds(0, MAIN)],
            xbuf.at[pl.ds(c * CH, CH), cols(x)],
            xs.at[d, c], xr.at[d, c], {"head": side[d]},
        )

    def main_fwd(d, c):
        half = xbuf.at[pl.ds(c * CH + d * (CH // 2), CH // 2), cols(side[1 - d])]
        return rcopy(half, half, fs.at[d, c], fr.at[d, c], {"head": side[d]})

    def tail_copy(d, s):
        part = tbuf.at[x, pl.ds(s * 256, 256), :]
        return rcopy(part, part, ts.at[d, s], tr.at[d, s], {"head": side[d]})

    def tail_fwd(d, s):
        part = tbuf.at[side[1 - d], pl.ds(s * 256 + d * 128, 128), :]
        return rcopy(part, part, us.at[d, s], ur.at[d, s], {"head": side[d]})

    def both(f, c, act):
        for d in range(2):
            getattr(f(d, c), act)()

    both(main_copy, 0, "start")
    stage_copy.wait()
    for s in range(2):
        lo = stage[s, pl.ds(0, 256), pl.ds(MAIN, TAIL)].astype(F32)
        hi = stage[s, pl.ds(256, 256), pl.ds(MAIN, TAIL)].astype(F32)
        gap = jnp.zeros((256, 16), F32)
        tbuf[x, pl.ds(s * 256, 256), :] = jnp.concatenate([lo, gap, hi, gap], axis=1).astype(BF16)
    both(tail_copy, 0, "start")
    both(main_copy, 1, "start")

    for c in wcopies:
        c.wait()
    lane = lax.broadcasted_iota(jnp.int32, (LN, LN), 1)

    def spread(b, _):
        r = pl.ds(pl.multiple_of(b * LN, LN), LN)
        for p in range(3):
            block = raw[p, r, :].astype(F32)
            for h in range(NH):
                piece = jnp.concatenate(
                    [block[:, h * HD : (h + 1) * HD], jnp.zeros((LN, LN - HD), F32)], axis=1
                )
                wcat[r, pl.ds(p * PW + h * LN, LN)] = piece.astype(BF16)
        return _

    lax.fori_loop(0, KW // LN, spread, 0)
    for i in range(NX):
        wcat[pl.ds(NX * MAIN + i * 64 + TAIL, 16), :] = jnp.zeros((16, 3 * PW), BF16)
    for c in own:
        c.wait()

    def tails(s):
        for half in range(2):
            for pair in range(2):
                a = tbuf[2 * pair, pl.ds(s * 256, 256), :].astype(F32)
                b = tbuf[2 * pair + 1, pl.ds(s * 256, 256), :].astype(F32)
                o = 64 * half
                tile = jnp.concatenate([a[:, o : o + 64], b[:, o : o + 64]], axis=1)
                xbuf[pl.ds(s * TOK + half * 256, 256), pl.ds(NX * MAIN + pair * LN, LN)] = tile.astype(BF16)

    def project(c):
        rows = pl.ds(c * CH, CH)

        def piece(first, relu):
            def body(n, _):
                w = pl.ds(pl.multiple_of(n * 256, 256), 256)
                r = jnp.dot(xbuf[rows, :], wcat[:, w], preferred_element_type=F32)
                if relu:
                    r = jnp.maximum(r, 0.0)
                qkv[rows, w] = r.astype(BF16)
                return _

            return body

        lax.fori_loop(0, 5, piece(0, True), 0)
        lax.fori_loop(5, 7, piece(5, False), 0)
        w = pl.ds(7 * 256, LN)
        qkv[rows, w] = jnp.dot(xbuf[rows, :], wcat[:, w], preferred_element_type=F32).astype(BF16)

    def states(s):
        rows = pl.ds(s * TOK, TOK)
        for h in range(NH):
            k = qkv[rows, pl.ds(h * LN, LN)]
            v = qkv[rows, pl.ds(2 * PW + h * LN, LN)]
            r = lax.dot_general(k, v, (((0,), (0,)), ((), ())), preferred_element_type=F32)
            st32[s, pl.ds(h * LN, LN), :] = r
            st16[s, pl.ds(h * LN, LN), :] = r.astype(BF16)

    def quarter(i):
        return pl.ds(pl.multiple_of(i * QR, QR), QR)

    def scatter(s, d):
        to = (y + d) % NY
        return rcopy(
            st16.at[s, quarter(to), :], rsbuf.at[s, d - 1], ys.at[s, d - 1], yr.at[s, d - 1], {"tok": to}
        )

    def collect(s):
        total = st32[s, quarter(y), :]
        for d in range(1, NY):
            scatter(s, d).wait_recv()
            total = total + rsbuf[s, d - 1].astype(F32)
        return total

    def gather(s, d):
        part = tot.at[s, quarter(y), :]
        return rcopy(part, part, ys.at[2 + s, d - 1], yr.at[2 + s, d - 1], {"tok": (y + d) % NY})

    core_copy = rcopy(csend, crecv, cs.at[0], cr.at[0], {"group": mate})
    pre_copy = rcopy(psend, precv, cs.at[1], cr.at[1], {"group": mate})

    def zcopy(d):
        return rcopy(
            zsend, zrecv.at[d - 1], zs.at[d - 1], zr.at[d - 1], {"group": ((z + d) % NZ) * 2 + core}
        )

    def eighth(i):
        return pl.ds(pl.multiple_of(i * ER, ER), ER)

    def read(s):
        for h in range(NH):
            pass
        for t in range(TOK // CH):
            rows = pl.ds(s * TOK + t * CH, CH)
            heads = []
            for h in range(NH):
                q = qkv[rows, pl.ds(PW + h * LN, LN)]
                r = jnp.dot(q, tot[s, pl.ds(h * LN, LN), :], preferred_element_type=F32)
                mean = jnp.sum(r * r, axis=1, keepdims=True) * (1.0 / HD)
                r = r * lax.rsqrt(mean + 1e-06)
                heads.append(r[:, :HD])
            packed = jnp.concatenate(heads, axis=1) * gain[...]
            obuf[s, pl.ds(t * CH, CH), :] = packed.astype(BF16)

    def chain(step):
        if step == 4:
            cst[...] = collect(0)
            csend[...] = cst[...].astype(BF16)
            core_copy.start()
        elif step == 5:
            core_copy.wait_recv()
            zsend[...] = (cst[eighth(core), :] + crecv[eighth(core), :].astype(F32)).astype(BF16)
            for d in range(1, NZ):
                zcopy(d).start()
        elif step == 6:
            acc = jnp.zeros((ER, LN), F32)
            for d in range(1, NZ):
                zcopy(d).wait_recv()
                acc = acc + jnp.where(z >= d, zrecv[d - 1].astype(F32), 0.0)
            pfx[eighth(core), :] = acc
            psend[...] = acc.astype(BF16)
            pre_copy.start()
        elif step == 7:
            pre_copy.wait_recv()
            pfx[eighth(1 - core), :] = precv[...].astype(F32)
            pfx[...] = pfx[...] + jnp.where(core == 1, crecv[...].astype(F32), 0.0)
            tot[0, quarter(y), :] = (pfx[...] + cst[...]).astype(BF16)
            for d in range(1, NY):
                gather(0, d).start()

    half = NC // 2
    for c in range(NC + 1):
        if c < NC:
            both(main_copy, c, "wait_recv")
            both(main_fwd, c, "start")
            if c % half == 0:
                both(tail_copy, c // half, "wait_recv")
                both(tail_fwd, c // half, "start")
            if c + 2 < NC:
                if c + 2 == half:
                    both(tail_copy, 1, "start")
                both(main_copy, c + 2, "start")
        if c >= 1:
            b = c - 1
            if b % half == 0:
                both(tail_fwd, b // half, "wait_recv")
                tails(b // half)
            both(main_fwd, b, "wait_recv")
            project(b)
            if b == half - 1:
                states(0)
                for d in range(1, NY):
                    scatter(0, d).start()
            chain(b)
    states(1)
    for d in range(1, NY):
        scatter(1, d).start()
    for d in range(1, NY):
        gather(0, d).wait_recv()
    read(0)
    out_copies = [pltpu.make_async_copy(obuf.at[s], out.at[s], osem.at[s]) for s in range(2)]
    out_copies[0].start()
    tot[1, quarter(y), :] = (collect(1) + pfx[...]).astype(BF16)
    for d in range(1, NY):
        gather(1, d).start()
    for d in range(1, NY):
        gather(1, d).wait_recv()
    read(1)
    out_copies[1].start()

    for c in range(NC):
        both(main_copy, c, "wait_send")
        both(main_fwd, c, "wait_send")
    for s in range(2):
        both(tail_copy, s, "wait_send")
        both(tail_fwd, s, "wait_send")
        for d in range(1, NY):
            scatter(s, d).wait_send()
            gather(s, d).wait_send()
    core_copy.wait_send()
    pre_copy.wait_send()
    for d in range(1, NZ):
        zcopy(d).wait_send()
    for c in out_copies:
        c.wait()


def local(streams, w_query, w_key, w_value, gain):
    any_spec = pl.BlockSpec(memory_space=pl.ANY)
    vmem = pltpu.VMEM
    dma = pltpu.SemaphoreType.DMA
    return pl.pallas_call(
        kernel,
        out_shape=jax.ShapeDtypeStruct(streams.shape, BF16),
        in_specs=[any_spec] * 4 + [pl.BlockSpec(memory_space=pltpu.VMEM)],
        out_specs=any_spec,
        scratch_shapes=[
            vmem((3, KW, DW), BF16),
            vmem((KW, 3 * PW), BF16),
            vmem((2, TOK, DW), BF16),
            vmem((ROWS, KW), BF16),
            vmem((NX, TOK, LN), BF16),
            vmem((ROWS, 3 * PW), BF16),
            vmem((2, TOK, DW), BF16),
            vmem((2, PW, LN), F32),
            vmem((2, PW, LN), BF16),
            vmem((2, NY - 1, QR, LN), BF16),
            vmem((QR, LN), F32),
            vmem((QR, LN), BF16),
            vmem((QR, LN), BF16),
            vmem((ER, LN), BF16),
            vmem((NZ - 1, ER, LN), BF16),
            vmem((ER, LN), BF16),
            vmem((ER, LN), BF16),
            vmem((QR, LN), F32),
            vmem((2, PW, LN), BF16),
            dma((3,)),
            dma((3, 2 * NX)),
            dma((2,)),
            dma((2, NC)), dma((2, NC)),
            dma((2, NC)), dma((2, NC)),
            dma((2, 2)), dma((2, 2)),
            dma((2, 2)), dma((2, 2)),
            dma((4, NY - 1)), dma((4, NY - 1)),
            dma((2,)), dma((2,)),
            dma((NZ - 1,)), dma((NZ - 1,)),
        ],
        compiler_params=pltpu.CompilerParams(
            collective_id=0, has_side_effects=True, vmem_limit_bytes=60 * 1024 * 1024
        ),
        name="linear_attention",
    )(streams, w_query, w_key, w_value, gain.reshape(1, DW))


def solution(mesh):
    return jax.shard_map(
        local,
        mesh=mesh,
        in_specs=(
            P(None, ("group", "tok"), "head"),
            P(None, "head"),
            P(None, "head"),
            P(None, "head"),
            P("head"),
        ),
        out_specs=P(None, ("group", "tok"), "head"),
        check_vma=False,
    )
```

time: 199 us -> 86.2 us (0.43)
  waiting for transfers between devices: 145 us -> 0 us
  Pallas kernels: 0 us -> 67.9 us
  matrix products: 18 us -> 0 us
  other arithmetic: 17 us -> 0 us
  local copies, waits for them, and re-layouts: 2.93 us -> 18.1 us
  between operations: 13.2 us -> 0.01 us
    all_gather x2 -> x0, waiting for transfers between devices: 95.5 us -> none  [the longest x1 58.5 us: local(): pieces = lax.all_gather(streams, 'head', axis=2, tiled=True)]
    pallas_call x0 -> x1, Pallas kernels: none -> 67.9 us  [local(): pl.pallas_call(kernel, out_shape=jax.ShapeDtypeStruct(streams.shape, BF16...]
    psum x1 -> x0, waiting for transfers between devices: 49.1 us -> none  [local(): clean_total, noisy_total = lax.psum((clean_part, noisy_part), 'tok')]
    dot_general x5 -> x0, matrix products: 18 us -> none  [the longest x3 15 us: local(): jnp.einsum('std,dw->stw', pieces, matrix, preferred_element_type=jnp.floa...]
    select_n x15 -> x0, other arithmetic: 15.6 us -> none  [lap(): return jnp.where(position < mine, longer, total)]
    unnamed x12 -> x6, local copies, waits for them, and re-layouts: 0.03 us -> 14.5 us
    pallas_call x0 -> x1, local copies, waits for them, and re-layouts: none -> 2.36 us  [local(): pl.pallas_call(kernel, out_shape=jax.ShapeDtypeStruct(streams.shape, BF16...]
  transfers between devices with their start and end apart: 3 -> 0, of which waited for: 3 -> 0; matrix products, arithmetic and copies ran while one was open for 4% -> 0% of each run, Pallas kernels for 0% -> 0%
where the time goes in v1:
time: 86.2 us; the launch traced here: 86 us
  Pallas kernels  67.9 us (79%)
  local copies, waits for them, and re-layouts  18.1 us (21%)
    pallas_call x1, Pallas kernels, local(): pl.pallas_call(kernel, out_shape=jax.ShapeDtypeStruct(streams.shape, BF16...  67.9 us
    unnamed x6, local copies, waits for them, and re-layouts  14.5 us
    pallas_call x1, local copies, waits for them, and re-layouts, local(): pl.pallas_call(kernel, out_shape=jax.ShapeDtypeStruct(streams.shape, BF16...  2.36 us

profile of v1, /device:TPU:32, one launch (start us, length us, event | category | flops | bytes accessed | tf_op | source)
XLA Modules:
  0.0 86.0 jit_solution(987821496663943723)
XLA Ops:
  0.0 1.3 %reshape.3.gain = f32[1,560]{1,0:T(1,128)} reshape(f32[560]{0:T(1024)} %param.9) | data formatting | bytes 4480 | tf_op jit(solution)/shard_map/reshape | solution.py:359
  1.3 2.4 %copy.6.streams = bf16[2,512,560]{2,1,0:T(8,128)(2,1)} copy(bf16[2,512,560]{1,2,0:T(8,128)(2,1)} %param.5) | data formatting | bytes 2293760 | tf_op args[0]
  3.7 0.0 copy-start
  3.7 4.6 %copy.7.wq = bf16[2240,560]{1,0:T(8,128)(2,1)} copy(bf16[2240,560]{0,1:T(8,128)(2,1)} %param.6) | data formatting | bytes 5017600 | tf_op args[1]
  8.3 0.0 copy-done
  8.3 2.9 %copy.8.wk = bf16[2240,560]{1,0:T(8,128)(2,1)} copy(bf16[2240,560]{0,1:T(8,128)(2,1)S(1)} %copy-done) | data formatting | bytes 5017600 | tf_op args[2]
  11.2 4.5 %copy.9.wv = bf16[2240,560]{1,0:T(8,128)(2,1)} copy(bf16[2240,560]{0,1:T(8,128)(2,1)} %param.8) | data formatting | bytes 5017600 | tf_op args[3]
  15.7 67.9 %linear_attention.1 = bf16[2,512,560]{2,1,0:T(8,128)(2,1)} custom-call(bf16[2,512,560]{2,1,0:T(8,128)(2,1)} %copy.6.streams, bf16[2240,560]{1,0:T(8,128)(2,1)} %copy.7.wq, bf16[2240,560]{1,0:T(8,128)(2,1)} %copy.8.wk, bf16[2240,560]{1,0:T(8,128)(2,1)} %copy.9.wv, f32[1,560]{1,0:T(1,128)} %reshape.3.gain), custom_call_target="tpu_custom_call" | custom-call | tf_op jit(solution)/shard_map/linear_attention/pallas_call | solution.py:319
  83.6 2.4 %copy.10 = bf16[2,512,560]{1,2,0:T(8,128)(2,1)} copy(bf16[2,512,560]{2,1,0:T(8,128)(2,1)} %linear_attention.1) | data formatting | bytes 2293760 | tf_op jit(solution)/shard_map/linear_attention/pallas_call | solution.py:319
Async XLA Ops:
  3.7 4.6 %copy-start = (bf16[2240,560]{0,1:T(8,128)(2,1)S(1)}, bf16[2240,560]{0,1:T(8,128)(2,1)}, u32[]{:S(2)}) copy-start(bf16[2240,560]{0,1:T(8,128)(2,1)} %param.7) | copy-start | bytes 7526404
